TPU v7x, 256 devices: a whole 4x4x8 slice. The times are simulated.
256 devices in a mesh: section: 8 (over z), expert: 32 (over x, y, core).
Axes of the slice: x: 4, y: 4, z: 8, core: 2. Of those that a mesh axis runs over, the one named last changes fastest.
Arguments:
- grad_out: bfloat16 [4096, 4096], P('expert', 'section'), may hold values from -6 to 6
- probs: float32 [4096, 8], P('expert'), may hold values from 0.05 to 0.4
- expert_ids: int32 [4096, 8], P('expert'), may hold values from 0 to 63, all different within a row; in each aligned block of 128 rows (0 to 127, 128 to 255, ...) at most 24 rows name the same one
- w_gate: bfloat16 [64, 1536, 4096], P('expert', 'section'), may hold values from -0.09375 to 0.09375
- w_up: bfloat16 [64, 1536, 4096], P('expert', 'section'), may hold values from -0.09375 to 0.09375
- w_down: bfloat16 [64, 1536, 4096], P('expert', 'section'), may hold values from -0.15625 to 0.15625
- saved_gate: bfloat16 [64, 1536, 768], P('expert', 'section'), may hold values from -3 to 3
- saved_up: bfloat16 [64, 1536, 768], P('expert', 'section'), may hold values from -3 to 3
Outputs:
- grad_in: bfloat16 [4096, 4096], P('expert', 'section')
- grad_probs: bfloat16 [4096, 8], P('expert')
Inputs may be any that keep to these rules, and one draw needn't show every extreme that they name: `expert_ids`: each token names 8 different experts. Within the tokens of one index of expert (aligned blocks of 128 tokens) no expert is named more than 24 times, a bound that some block reaches.
All inputs are finite; a program needn't handle non-finite values.
Results may differ from a plain program's by a relative error of at most 0.015.
Values may be sent and summed in bfloat16 or wider, within the bound.
A program may use at most 128 MiB of HBM per device.

v0:
```python
import jax
import jax.numpy as jnp
from jax import lax
from jax.sharding import PartitionSpec as P

TOPK = 8


def local(grad_out, probs, expert_ids, w_gate, w_up, w_down, saved_gate, saved_up):
    groups = lax.axis_size("expert")
    local_experts = w_gate.shape[0]
    expert_count = local_experts * groups
    slot_count = saved_gate.shape[2]
    capacity = slot_count // groups
    token_count = grad_out.shape[0]
    feature_share = grad_out.shape[1]
    picked = expert_ids.reshape(-1)
    onehot = (picked[:, None] == jnp.arange(expert_count, dtype=jnp.int32)[None, :]).astype(
        jnp.int32
    )
    before = jnp.cumsum(onehot, axis=0) - onehot
    position = jnp.sum(before * onehot, axis=1)
    slot = picked * capacity + position
    owner = jnp.arange(picked.shape[0], dtype=jnp.int32) // TOPK
    table = jnp.full((expert_count * capacity,), token_count, jnp.int32).at[slot].set(owner)
    full_rows = lax.all_gather(grad_out, "section", axis=1, tiled=True)
    padded = jnp.concatenate([full_rows, jnp.zeros((1, full_rows.shape[1]), jnp.bfloat16)], axis=0)
    outgoing = padded[table].reshape(expert_count, capacity, full_rows.shape[1])
    arrived = lax.all_to_all(outgoing, "expert", split_axis=0, concat_axis=1, tiled=True)
    hidden_grad = jnp.einsum("esd,efd->efs", arrived, w_down, preferred_element_type=jnp.float32)
    gate_act = saved_gate.astype(jnp.float32)
    up_act = saved_up.astype(jnp.float32)
    sigmoid_gate = jax.nn.sigmoid(gate_act)
    silu_gate = gate_act * sigmoid_gate
    router_part = jnp.sum(silu_gate * up_act * hidden_grad, axis=1)
    router_grad = lax.psum(router_part, "section").astype(jnp.bfloat16)
    gate_grad = (
        hidden_grad * up_act * sigmoid_gate * (1.0 + gate_act * (1.0 - sigmoid_gate))
    ).astype(jnp.bfloat16)
    up_grad = (hidden_grad * silu_gate).astype(jnp.bfloat16)
    term = jnp.einsum("efc,efs->esc", w_gate, gate_grad, preferred_element_type=jnp.float32)
    term = term + jnp.einsum("efc,efs->esc", w_up, up_grad, preferred_element_type=jnp.float32)
    shares = lax.psum_scatter(term.astype(jnp.bfloat16), "section", scatter_dimension=2, tiled=True)
    back_grad, back_router = (
        lax.all_to_all(shares, "expert", split_axis=1, concat_axis=0, tiled=True),
        lax.all_to_all(router_grad, "expert", split_axis=1, concat_axis=0, tiled=True),
    )
    rows = back_grad.reshape(expert_count * capacity, feature_share)[slot]
    weighted = (
        rows.astype(jnp.float32).reshape(token_count, TOPK, feature_share) * probs[:, :, None]
    )
    grad_in = jnp.sum(weighted, axis=1).astype(jnp.bfloat16)
    grad_probs = back_router.reshape(-1)[slot].reshape(token_count, TOPK)
    return (grad_in, grad_probs)


def solution(mesh):
    placed = (
        P("expert", "section"),
        P("expert", None),
        P("expert", None),
        P("expert", "section", None),
        P("expert", "section", None),
        P("expert", "section", None),
        P("expert", "section", None),
        P("expert", "section", None),
    )
    return jax.shard_map(
        local,
        mesh=mesh,
        in_specs=placed,
        out_specs=(P("expert", "section"), P("expert", None)),
        check_vma=False,
    )
```

profile of v0, /device:TPU:1, one launch (start us, length us, event | category | flops | bytes accessed | tf_op | source)
XLA Modules:
  0.0 454.7 jit_solution(9075502163950577890)
XLA Ops:
  7.2 0.7 all-gather.2.cloned.1.call-update
  8.0 0.9 copy.23
  9.1 0.7 fusion.16
  9.8 30.8 %reduce-window.6 = s32[64,8,128]{2,1,0:T(8,128)S(1)} reduce-window(s32[64,8,128]{2,1,0:T(8,128)} %fusion.16, s32[]{:T(128)} %constant.30.clone.1), window={size=1x1x128 pad=0_0x0_0x127_0}, to_apply=%region_0.0 | reduce-window | flops 8323072 | bytes 524292 | tf_op jit(solution)/shard_map/reduce-window
  40.7 0.9 slice.14
  41.5 1.1 copy.25
  43.2 4.3 scatter_custom_fusion
  47.6 2.4 concatenate.3
  50.0 23.4 %gather_fusion = bf16[1536,4096]{1,0:T(8,128)(2,1)} fusion(bf16[129,4096]{1,0:T(8,128)(2,1)} %concatenate.3, s32[2048]{0:T(1024)S(1)} %pad_clamp_fusion), kind=kCustom, calls=%fused_computation | custom fusion | bytes 25171968 | tf_op jit(solution)/shard_map/gather | solution.py:28
  73.4 152.6 %all_to_all.49 = bf16[64,24,4096]{2,1,0:T(8,128)(2,1)S(1)} all-to-all(bf16[64,24,4096]{2,1,0:T(8,128)(2,1)} %bitcast.40), channel_id=1, replica_groups=mesh['section'=8,'expert'=32] {'expert'}, dimensions={0} | all-to-all | bytes 25165824 | tf_op jit(solution)/shard_map/all_to_all | solution.py:29
  226.0 5.2 %copy.27 = bf16[2,32,24,4096]{3,2,1,0:T(8,128)(2,1)} copy(bf16[2,32,24,4096]{3,2,0,1:T(8,128)(2,1)S(1)} %bitcast.41) | data formatting | bytes 25165824 | tf_op jit(solution)/shard_map/all_to_all | solution.py:29
  231.1 11.1 %fusion.5 = (f32[2,768]{1,0:T(2,128)S(1)}, f32[2,192,768]{2,1,0:T(8,128)}) fusion(bf16[2,192,768]{2,1,0:T(8,128)(2,1)} %param.15, bf16[2,192,768]{2,1,0:T(8,128)(2,1)} %param.14, bf16[2,768,4096]{2,1,0:T(8,128)(2,1)} %bitcast.42, bf16[2,192,4096]{2,1,0:T(8,128)(2,1)} %param.13), kind=kOutput, calls=%fused_computation.17 | convolution fusion | flops 2418571776 | bytes 18094080 | tf_op jit(solution)/shard_map/esd,efd->efs/dot_general | solution.py:30
  242.2 11.8 %fusion.10 = f32[2,768,4096]{2,1,0:T(8,128)} fusion(bf16[2,192,4096]{2,1,0:T(8,128)(2,1)S(1)} %copy-done, f32[2,192,768]{2,1,0:T(8,128)} %get-tuple-element.7, bf16[2,192,768]{2,1,0:T(8,128)(2,1)} %param.15, bf16[2,192,768]{2,1,0:T(8,128)(2,1)} %param.14), kind=kOutput, calls=%fused_computation.23 | convolution fusion | flops 2419458048 | bytes 30670848 | tf_op jit(solution)/shard_map/efc,efs->esc/dot_general | solution.py:41
  254.1 16.5 %add_convert_fusion = bf16[2,768,4096]{2,1,0:T(8,128)(2,1)} fusion(f32[2,768,4096]{2,1,0:T(8,128)} %fusion.10, bf16[2,192,4096]{2,1,0:T(8,128)(2,1)} %param.12, f32[2,192,768]{2,1,0:T(8,128)} %get-tuple-element.7, bf16[2,192,768]{2,1,0:T(8,128)(2,1)} %param.14), kind=kOutput, calls=%fused_computation.4 | convolution fusion | flops 2430566400 | bytes 42663936 | tf_op jit(solution)/shard_map/efc,efs->esc/dot_general | solution.py:42
  270.6 14.2 %psum.7 = bf16[2,768]{1,0:T(2,128)(2,1)S(1)} all-reduce(f32[2,768]{1,0:T(2,128)S(1)} %get-tuple-element.6), channel_id=1, replica_groups=mesh['section'=8,'expert'=32] {'section'}, use_global_device_ids=true, to_apply=%region_7.8 | all-reduce | flops 1536 | bytes 9216 | tf_op jit(solution)/shard_map/psum | solution.py:36
  285.5 6.8 %all-to-all-start.2 = ((bf16[2,32,24]{2,0,1:T(2,128)(2,1)}), bf16[2,32,24]{2,0,1:T(2,128)(2,1)S(1)}, u32[]{:S(2)}, u32[]{:S(2)}) async-start(bf16[2,32,24]{2,0,1:T(2,128)(2,1)} %copy.31), calls=%async_computation.3 | async-start | bytes 32768 | tf_op jit(solution)/shard_map/all_to_all | solution.py:46
  292.3 108.8 %reduce-scatter.2.cloned.1.call-done = bf16[2,768,512]{2,1,0:T(8,128)(2,1)} async-done(((bf16[2,768,4096]{2,1,0:T(8,128)(2,1)}), bf16[2,768,512]{2,1,0:T(8,128)(2,1)}) %reduce-scatter.2.cloned.1.call-update) | async-done | bytes 1572880 | tf_op jit(solution)/shard_map/reduce_scatter | solution.py:43
  401.1 4.2 copy.28
  405.3 7.6 %all-to-all-start.1 = ((bf16[2,768,512]{2,0,1:T(2,128)(2,1)}), bf16[2,768,512]{2,0,1:T(2,128)(2,1)}, u32[]{:S(2)}, u32[]{:S(2)}) async-start(bf16[2,768,512]{2,0,1:T(2,128)(2,1)} %copy.28), calls=%async_computation.2 | async-start | bytes 3145728 | tf_op jit(solution)/shard_map/all_to_all | solution.py:45
  413.1 6.8 %gather_fusion.2 = bf16[1024]{0:T(1024)(128)(2,1)S(1)} fusion(bf16[1536]{0:T(1024)(128)(2,1)S(1)} %reshape.75, s32[1024]{0:T(1024)S(1)} %broadcast_clamp_fusion), kind=kCustom, calls=%fused_computation.2 | custom fusion | bytes 8192 | tf_op jit(solution)/shard_map/gather | solution.py:53
  420.7 14.9 %all-to-all-done.1 = bf16[2,768,512]{2,0,1:T(2,128)(2,1)} async-done(((bf16[2,768,512]{2,0,1:T(2,128)(2,1)}), bf16[2,768,512]{2,0,1:T(2,128)(2,1)}, u32[]{:S(2)}, u32[]{:S(2)}) %all-to-all-start.1) | async-done | bytes 1572896 | tf_op jit(solution)/shard_map/all_to_all | solution.py:45
  435.6 2.9 copy.29
  438.5 6.7 %gather_fusion.1 = bf16[1024,512]{1,0:T(8,128)(2,1)} fusion(bf16[1536,512]{1,0:T(8,128)(2,1)} %bitcast.39, s32[1024]{0:T(1024)S(1)} %broadcast_clamp_fusion), kind=kCustom, calls=%fused_computation.1 | custom fusion | bytes 2101248 | tf_op jit(solution)/shard_map/gather | solution.py:48
  445.2 2.6 fusion
  (32 shorter events, 2.5 us)
Async XLA Ops:
  7.2 235.1 %copy-start = (bf16[2,192,4096]{2,1,0:T(8,128)(2,1)S(1)}, bf16[2,192,4096]{2,1,0:T(8,128)(2,1)}, u32[]{:S(2)}) copy-start(bf16[2,192,4096]{2,1,0:T(8,128)(2,1)} %param.11) | copy-start | bytes 9437188
  7.2 35.6 %copy-start.1 = (s32[128,8]{0,1:T(8,128)S(1)}, s32[128,8]{0,1:T(8,128)}, u32[]{:S(2)}) copy-start(s32[128,8]{0,1:T(8,128)} %param.10) | copy-start | bytes 12292
  7.2 40.4 %all-gather.2.cloned.1.call-start = ((), (), s32[]{:S(2)}) async-start(), calls=%async_computation.4 | async-start | bytes 1179648 | tf_op jit(solution)/shard_map/all_gather | solution.py:26
  7.9 393.2 %reduce-scatter.2.cloned.1.call-start = ((), (), s32[]{:S(2)}) async-start(), calls=%async_computation.5 | async-start | bytes 14155776 | tf_op jit(solution)/shard_map/reduce_scatter | solution.py:43
  285.5 119.8 %all-to-all-start.2 = ((bf16[2,32,24]{2,0,1:T(2,128)(2,1)}), bf16[2,32,24]{2,0,1:T(2,128)(2,1)S(1)}, u32[]{:S(2)}, u32[]{:S(2)}) async-start(bf16[2,32,24]{2,0,1:T(2,128)(2,1)} %copy.31), calls=%async_computation.3 | async-start | bytes 32768 | tf_op jit(solution)/shard_map/all_to_all | solution.py:46
  405.3 7.6 %copy-start.2 = (f32[128,8]{0,1:T(8,128)S(1)}, f32[128,8]{0,1:T(8,128)}, u32[]{:S(2)}) copy-start(f32[128,8]{0,1:T(8,128)} %param.9) | copy-start | bytes 12292
  405.3 30.3 %all-to-all-start.1 = ((bf16[2,768,512]{2,0,1:T(2,128)(2,1)}), bf16[2,768,512]{2,0,1:T(2,128)(2,1)}, u32[]{:S(2)}, u32[]{:S(2)}) async-start(bf16[2,768,512]{2,0,1:T(2,128)(2,1)} %copy.28), calls=%async_computation.2 | async-start | bytes 3145728 | tf_op jit(solution)/shard_map/all_to_all | solution.py:45
Sparse Core Ops, SparseCore 0:
  9.8 37.5 all-gather.1
  270.7 130.3 reduce-scatter.1
where the time goes:
time: 457 us; the launch traced here: 455 us
  blocking collectives  167 us (37%)
  waiting for transfers between devices  124 us (27%)
  local copies, waits for them, and re-layouts  60.9 us (13%)
  matrix products  39.4 us (9%)
  other arithmetic  34.4 us (8%)
  starting transfers between devices  14.5 us (3%)
  between operations  14.2 us (3%)
    all_to_all x1, blocking collectives, local(): lax.all_to_all(outgoing, 'expert', split_axis=0, concat_axis=1, tiled=True)  153 us
    reduce_scatter x1, waiting for transfers between devices, local(): lax.psum_scatter(term.astype(jnp.bfloat16), 'section', scatter_dimension=...  109 us
    another operation x3, other arithmetic  31 us
    gather x1, local copies, waits for them, and re-layouts, local(): outgoing = padded[table].reshape(expert_count, capacity, full_rows.shape[1])  23.4 us
    dot_general x1, matrix products, local(): jnp.einsum('efc,efs->esc', w_up, up_grad, preferred_element_type=jnp.floa...  16.5 us
    all_to_all x1, waiting for transfers between devices, local(): lax.all_to_all(shares, 'expert', split_axis=1, concat_axis=0, tiled=True)  14.9 us
    psum x1, blocking collectives, local(): router_grad = lax.psum(router_part, 'section').astype(jnp.bfloat16)  14.2 us
    dot_general x1, matrix products, local(): jnp.einsum('efc,efs->esc', w_gate, gate_grad, preferred_element_type=jnp....  11.8 us
  transfers between devices with their start and end apart: 4, of which 2 were waited for; matrix products, arithmetic and copies ran while one was open for 11% of the time, Pallas kernels for 0%

commit v1 on v0

v1 whole, which is shorter than its diff:
```python
import jax
import jax.numpy as jnp
from jax import lax
from jax.experimental import pallas as pl
from jax.experimental.pallas import tpu as pltpu
from jax.sharding import PartitionSpec as P

TOPK = 8
NZ = 8
CAP = 24
TB = 128
MESH = pl.DeviceIdType.MESH
F32 = jnp.float32
BF16 = jnp.bfloat16


def kernel(
    ids_ref, probs_ref, x_hbm, wg_hbm, wu_hbm, wd_hbm, sg_hbm, su_hbm,
    out_ref, gp_ref,
    tok, wg, wu, wd, sg, su, down, dpar, sendbuf, part, rbuf, fin, back,
    idsall, masks, codes, rown, rrecv, rcol, whi, wlo, onehot, ggs, ugs,
    ld_sem, x_sem, zs_sem, zr_sem, ids_s, ids_r, st1_s, fw1_s, st2_s, fw2_s, tok_r,
    dp_s, dp_r, rs_s, rs_r, rt_s, rt_r, bk_s, bk_r,
):
    z = lax.axis_index("section")
    e = lax.axis_index("expert")
    x, y, c = e // 8, (e // 2) % 4, e % 2
    partner = e + 1 - 2 * c
    zp, zm = (z + 1) % NZ, (z + NZ - 1) % NZ
    D = tok.shape[2]
    DS = D // NZ
    F = wd.shape[1]

    def dev(cc, i, j):
        ax = (x * (1 - cc) + y * cc + i) % 4
        ay = (y * (1 - cc) + x * cc + j) % 4
        return ((ax * (1 - cc) + ay * cc) * 4 + (ay * (1 - cc) + ax * cc)) * 2 + cc

    def gray(m):
        return m + (m // 2) * (1 - 2 * (m % 2))

    def place(k, m):
        mid = (k * (3 - k)) // 2
        v = 2 * ((k + 2) % 3) + m // 2
        i = gray(m) * (1 - mid) + gray(v) * mid
        j = 2 * (k // 3) * (1 - mid) + (1 + 2 * (m % 2)) * mid
        return i, j

    def rcopy(src, dst, ssem, rsem, zz, ee):
        return pltpu.make_async_remote_copy(
            src_ref=src, dst_ref=dst, send_sem=ssem, recv_sem=rsem,
            device_id=(zz, ee), device_id_type=MESH,
        )

    def cols(q):
        return pl.ds(pl.multiple_of(q * DS, DS), DS)

    xcopy = pltpu.make_async_copy(x_hbm, tok.at[0, :, cols(z)], x_sem)
    xcopy.start()
    loads = [
        pltpu.make_async_copy(a, b, ld_sem.at[n])
        for n, (a, b) in enumerate(
            ((sg_hbm, sg), (su_hbm, su), (wd_hbm, wd), (wg_hbm, wg), (wu_hbm, wu))
        )
    ]
    idcopy = pltpu.make_async_copy(ids_ref, idsall.at[0], ld_sem.at[5])
    idcopy.start()

    barrier = pltpu.get_barrier_semaphore()

    def greet_z(n, carry):
        pl.semaphore_signal(barrier, inc=1, device_id=((z + n) % NZ, e), device_id_type=MESH)
        return carry

    def greet_e(n, carry):
        pl.semaphore_signal(barrier, inc=1, device_id=(z, (e + n) % 32), device_id_type=MESH)
        return carry

    lax.fori_loop(1, NZ, greet_z, 0)
    lax.fori_loop(1, 32, greet_e, 0)
    pl.semaphore_wait(barrier, NZ - 1 + 31)

    xcopy.wait()
    idcopy.wait()

    a1p, a1m = dev(c, 1, 0), dev(c, 3, 0)
    a2p, a2m = dev(c, 0, 1), dev(c, 0, 3)
    half = TB // 2

    def zpiece(q, rows):
        return tok.at[0, rows, cols(q)]

    full, lo, hi = pl.ds(0, TB), pl.ds(0, half), pl.ds(half, half)

    def zsend(d, s):
        q = (z + NZ - s) % NZ if d == 0 else (z + s) % NZ
        rows = full if s < 3 else (lo if d == 0 else hi)
        return rcopy(
            zpiece(q, rows), zpiece(q, rows), zs_sem.at[d, s], zr_sem.at[d, s],
            zp if d == 0 else zm, e,
        )

    def zrecv(d, s):
        q = (z + NZ - 1 - s) % NZ if d == 0 else (z + 1 + s) % NZ
        rows = full if s < 3 else (lo if d == 0 else hi)
        return rcopy(
            zpiece(q, rows), zpiece(q, rows), zs_sem.at[d, s], zr_sem.at[d, s],
            zp if d == 0 else zm, e,
        )

    def first(q):
        rcopy(tok.at[0, :, cols(q)], tok.at[2, :, cols(q)], st1_s.at[0], tok_r.at[2, 0], z, a1p).start()
        rcopy(tok.at[0, :, cols(q)], tok.at[1, :, cols(q)], st1_s.at[1], tok_r.at[1, 0], z, a1m).start()

    zsend(0, 0).start()
    zsend(1, 0).start()

    def send_ids(n, carry):
        i, j = n // 4, n % 4
        mi, jj = gray((4 - i) % 4), (4 - j) % 4
        odd = jj % 2
        slot = (1 - odd) * (6 * jj + mi) + odd * (4 + 2 * mi + jj // 2)
        rcopy(idsall.at[0], idsall.at[slot], ids_s, ids_r, z, dev(c, i, j)).start()
        return carry

    lax.fori_loop(1, 16, send_ids, 0)
    first(z)
    for cp in loads:
        cp.start()
    for s in range(1, 4):
        zrecv(0, s - 1).wait_recv()
        zsend(0, s).start()
        zrecv(1, s - 1).wait_recv()
        zsend(1, s).start()
        first((z + NZ - s) % NZ)
        first((z + s) % NZ)
    zrecv(0, 3).wait_recv()
    zrecv(1, 3).wait_recv()
    first((z + 4) % NZ)

    rcopy(idsall.at[1:16], idsall.at[1:16], ids_s, ids_r, z, a1p).wait_recv()
    row8 = lax.broadcasted_iota(jnp.int32, (8, TB), 0)
    mine = jnp.where(row8 < 2, 2 * e + row8, 2 * partner + row8 - 2)
    mine = jnp.where(row8 < 4, mine, -1)

    def mask_of(n, carry):
        table = idsall[n]
        hit = jnp.zeros((8, TB), F32)
        for k in range(TOPK):
            hit = hit + jnp.where(table[k : k + 1, :] == mine, 1.0, 0.0)
        masks[n] = hit
        return carry

    lax.fori_loop(0, 16, mask_of, 0)
    r128 = lax.broadcasted_iota(jnp.int32, (TB, TB), 0)
    l128 = lax.broadcasted_iota(jnp.int32, (TB, TB), 1)
    tri = jnp.where(r128 < l128, 1.0, 0.0).astype(BF16)
    mk = masks[...].reshape(TB, TB)
    ps = jnp.dot(mk.astype(BF16), tri, preferred_element_type=F32)
    codes[...] = jnp.where(mk > 0.5, ps, -1.0).reshape(16, 8, TB)

    hit = jnp.zeros((TB, TB), F32)
    pe = jnp.zeros((TB, TB), F32)
    for k in range(TOPK):
        same = ids_ref[k : k + 1, :] == r128
        hit = hit + jnp.where(same, 1.0, 0.0)
        pe = pe + jnp.where(same, probs_ref[k : k + 1, :], 0.0)
    ps = jnp.dot(hit.astype(BF16), tri, preferred_element_type=F32)
    code_te = jnp.where(hit > 0.5, ps, -1.0).T.astype(BF16)
    prob_te = pe.T
    prob_hi = prob_te.astype(BF16)
    prob_lo = (prob_te - prob_hi.astype(F32)).astype(BF16)
    LT = onehot.shape[1]
    for lt in range(0, LT, 512):
        el = lax.broadcasted_iota(jnp.int32, (TB, 512), 0)
        ll = lax.broadcasted_iota(jnp.int32, (TB, 512), 1) + lt
        off = ll - CAP * el
        spread = jnp.where((off >= 0) & (off < CAP), 1.0, 0.0)
        s_of = jnp.sum(spread * off.astype(F32), axis=0, keepdims=True)
        spread = spread.astype(BF16)
        code_l = jnp.dot(code_te, spread, preferred_element_type=F32)
        prob_l = jnp.dot(prob_hi, spread, preferred_element_type=F32) + jnp.dot(
            prob_lo, spread, preferred_element_type=F32
        )
        oh = jnp.where(jnp.abs(code_l - s_of) < 0.5, 1.0, 0.0)
        w = oh * prob_l
        w_hi = w.astype(BF16)
        onehot[:, lt : lt + 512] = oh.astype(BF16)
        whi[:, lt : lt + 512] = w_hi
        wlo[:, lt : lt + 512] = (w - w_hi.astype(F32)).astype(BF16)

    def second(mi):
        rcopy(tok.at[mi], tok.at[5 + 2 * mi], st2_s.at[mi, 0], tok_r.at[5 + 2 * mi, 0], z, a2p).start()
        rcopy(tok.at[mi], tok.at[4 + 2 * mi], st2_s.at[mi, 1], tok_r.at[4 + 2 * mi, 0], z, a2m).start()

    def whole(n):
        return rcopy(tok.at[n], tok.at[n], st2_s.at[0, 0], tok_r.at[n, 0], z, a2p)

    def half_of(n, h):
        rows = pl.ds(h * half, half)
        return rcopy(tok.at[n, rows], tok.at[n, rows], st2_s.at[0, 0], tok_r.at[n, h], z, a2p)

    fwd1_hi = rcopy(tok.at[1, hi], tok.at[3, hi], fw1_s.at[1], tok_r.at[3, 1], z, a1m)
    fwd1_lo = rcopy(tok.at[2, lo], tok.at[3, lo], fw1_s.at[0], tok_r.at[3, 0], z, a1p)
    whole(1).wait_recv()
    fwd1_hi.start()
    whole(2).wait_recv()
    fwd1_lo.start()
    second(0)
    second(1)
    second(2)
    for cp in loads:
        cp.wait()

    def arrive(it, m):
        @pl.when((it >= 1) & (it <= 2))
        def _():
            n = 4 * it + m
            u = 4 * (it - 1) + m
            whole(n).wait_recv()
            jj = m % 2
            rows = pl.ds((1 - jj) * half, half)
            n2 = 12 + u // 2
            rcopy(
                tok.at[n, rows], tok.at[n2, rows], fw2_s.at[u], tok_r.at[n2, 1 - jj],
                z, a2p if jj == 1 else a2m,
            ).start()

        @pl.when(it == 3)
        def _():
            half_of(12 + m, 0).wait_recv()
            half_of(12 + m, 1).wait_recv()

    s24 = lax.broadcasted_iota(jnp.int32, (CAP, TB), 0).astype(F32)

    def dsend(k, pair, ee):
        return rcopy(
            sendbuf.at[pair, ee], dpar.at[k, ee, pair], dp_s.at[pair, ee], dp_r.at[k, ee, pair],
            z, partner,
        )

    def dispatch(it, pair):
        n0 = 4 * it + 2 * pair
        code0, code1 = codes[n0], codes[n0 + 1]
        zero = jnp.zeros((CAP, TB), F32)
        blocks = []
        for q in range(4):
            b0 = jnp.where(jnp.abs(code0[q : q + 1, :] - s24) < 0.5, 1.0, 0.0)
            b1 = jnp.where(jnp.abs(code1[q : q + 1, :] - s24) < 0.5, 1.0, 0.0)
            blocks.append(jnp.concatenate([b0, zero], axis=1))
            blocks.append(jnp.concatenate([zero, b1], axis=1))
        pick = jnp.concatenate(blocks, axis=0).astype(BF16)

        @pl.when(it >= 1)
        def _():
            dsend(it - 1, pair, 0).wait_send()
            dsend(it - 1, pair, 1).wait_send()

        def tile(t, carry):
            cs = pl.ds(pl.multiple_of(t * 512, 512), 512)
            rows = tok[pl.ds(n0, 2), :, cs].reshape(2 * TB, 512)
            got = jnp.dot(pick, rows, preferred_element_type=F32).astype(BF16)
            down[0, pair, :, cs] = got[0:48]
            down[1, pair, :, cs] = got[48:96]
            sendbuf[pair, 0, :, cs] = got[96:144]
            sendbuf[pair, 1, :, cs] = got[144:192]
            return carry

        lax.fori_loop(0, D // 512, tile, 0)
        dsend(it, pair, 0).start()
        dsend(it, pair, 1).start()

    NT = (((1,), (1,)), ((), ()))

    def saved_rows(it):
        base = lax.broadcasted_iota(jnp.int32, (CAP, sg.shape[2]), 1) - lax.broadcasted_iota(
            jnp.int32, (CAP, sg.shape[2]), 0
        )
        blocks = []
        for o in range(2):
            cc = c if o == 0 else 1 - c
            for m in range(4):
                i, j = place(it, m)
                blocks.append(jnp.where(base == dev(cc, i, j) * CAP, 1.0, 0.0))
        return jnp.concatenate(blocks, axis=0).astype(BF16)

    def hidden(it, ee, perm, eye):
        acc = jnp.zeros((192, F), F32)
        for kt in range(0, D, 512):
            rows = jnp.concatenate(
                [
                    down[ee, :, :, kt : kt + 512].reshape(96, 512),
                    dpar[it, ee, :, :, kt : kt + 512].reshape(96, 512),
                ],
                axis=0,
            )
            acc = acc + lax.dot_general(
                rows, wd[ee, :, kt : kt + 512], NT, preferred_element_type=F32
            )
        g = lax.dot_general(perm, sg[ee], NT, preferred_element_type=F32)
        u = lax.dot_general(perm, su[ee], NT, preferred_element_type=F32)
        s = 1.0 / (1.0 + jnp.exp(-g))
        silu = g * s
        router = jnp.sum(silu * u * acc, axis=1, keepdims=True)
        rown[it, ee : ee + 1, 0:192] = jnp.sum(router * eye, axis=0, keepdims=True)
        ggs[ee] = (acc * u * s * (1.0 + g * (1.0 - s))).astype(BF16)
        ugs[ee] = (acc * silu).astype(BF16)

    def eye_of():
        return jnp.where(
            lax.broadcasted_iota(jnp.int32, (192, 192), 0)
            == lax.broadcasted_iota(jnp.int32, (192, 192), 1),
            1.0,
            0.0,
        )

    def rs_wait_send(buf, ee):
        rcopy(
            part.at[buf, ee, 0:7], part.at[buf, ee, 0:7], rs_s.at[buf, ee], rs_r.at[0, 0, ee, 0],
            zp, e,
        ).wait_send()

    def partial(it, ee):
        buf = it % 2

        @pl.when(it >= 2)
        def _():
            rs_wait_send(buf, ee)

        gg, ug = ggs[ee], ugs[ee]

        def tile(t, carry):
            cs = cols(t)
            v = jnp.dot(gg, wg[ee, :, cs], preferred_element_type=F32) + jnp.dot(
                ug, wu[ee, :, cs], preferred_element_type=F32
            )
            part[buf, ee, t] = v.astype(BF16).reshape(4, 48, DS)
            return carry

        lax.fori_loop(0, NZ, tile, 0)

    def router_copy(k, n):
        return rcopy(rown.at[k], rrecv.at[k, n - 1], rt_s.at[k], rt_r.at[k], (z + n) % NZ, e)

    def send_router(it):
        def go(n, carry):
            router_copy(it, n).start()
            return carry

        lax.fori_loop(1, NZ, go, 0)

    def work(it, s):
        if s == 0:
            arrive(it, 0)
            arrive(it, 1)
            dispatch(it, 0)
        elif s == 1:
            arrive(it, 2)
        elif s == 2:
            @pl.when(it == 0)
            def _():
                half_of(3, 0).wait_recv()
                half_of(3, 1).wait_recv()
                second(3)

            arrive(it, 3)
            dispatch(it, 1)
        elif s == 3:
            for ee in range(2):
                for pair in range(2):
                    dsend(it, pair, ee).wait_recv()
            hidden(it, 0, saved_rows(it), eye_of())
        elif s == 4:
            hidden(it, 1, saved_rows(it), eye_of())
            send_router(it)
        elif s == 5:
            partial(it, 0)
        else:
            partial(it, 1)

    def rs_copy(k, s, ee, sub):
        t = (z + 2 * NZ - 1 - s) % NZ if ee == 0 else (z + 1 + s) % NZ
        return rcopy(
            part.at[k % 2, ee, t, sub], rbuf.at[k, s, ee, sub], rs_s.at[k % 2, ee],
            rs_r.at[k, s, ee, sub], zp if ee == 0 else zm, e,
        ), t

    def ring(k, s):
        def one(sub, carry):
            for ee in range(2):
                cp, t = rs_copy(k, s, ee, sub)
                if s:
                    rs_copy(k, s - 1, ee, sub)[0].wait_recv()
                    part[k % 2, ee, t, sub] = (
                        part[k % 2, ee, t, sub].astype(F32)
                        + rbuf[k, s - 1, ee, sub].astype(F32)
                    ).astype(BF16)
                cp.start()
            return carry

        lax.fori_loop(0, 4, one, 0)

    def message(n, cc, i, j):
        return rcopy(fin.at[n], back.at[e], bk_s, bk_r, z, dev(cc, i, j))

    def finish(k):
        rcopy(rrecv.at[k], rrecv.at[k], rt_s.at[k], rt_r.at[k], zp, e).wait()
        rows = rown[k]
        for n in range(NZ - 1):
            rows = rows + rrecv[k, n]
        eye = eye_of()
        for ee in range(2):
            col = jnp.sum(rows[ee : ee + 1, 0:192] * eye, axis=1, keepdims=True)
            rcol[ee] = jnp.broadcast_to(col, (192, 128)).reshape(4, 48, 128)

        def one(sub, carry):
            got = []
            for ee in range(2):
                rs_copy(k, NZ - 2, ee, sub)[0].wait_recv()
                got.append(
                    part[k % 2, ee, z, sub].astype(F32) + rbuf[k, NZ - 2, ee, sub].astype(F32)
                )
            o, pair = sub // 2, sub % 2
            cc = c * (1 - o) + (1 - c) * o
            for a in range(2):
                n = 8 * k + 2 * sub + a
                sl = slice(24 * a, 24 * a + 24)
                fin[n, :, 0:DS] = jnp.concatenate([got[0][sl], got[1][sl]], axis=0).astype(BF16)
                fin[n, :, DS : DS + 128] = jnp.concatenate(
                    [rcol[0, sub, sl], rcol[1, sub, sl]], axis=0
                ).astype(BF16)
                i, j = place(k, 2 * pair + a)
                if a == 0:
                    own = (k == 0) & (sub == 0)

                    @pl.when(own)
                    def _():
                        back[e] = fin[n]

                    @pl.when(jnp.logical_not(own))
                    def _():
                        message(n, cc, i, j).start()
                else:
                    message(n, cc, i, j).start()
            return carry

        lax.fori_loop(0, 4, one, 0)

    def step(it, carry):
        for s in range(7):
            @pl.when((it >= 1) & (it <= 4))
            def _():
                ring(it - 1, s)

            if s == 0:
                @pl.when(it >= 2)
                def _():
                    finish(it - 2)

            @pl.when(it <= 3)
            def _():
                work(it, s)

        return carry

    lax.fori_loop(0, 6, step, 0)

    rcopy(back.at[0:31], back.at[0:31], bk_s, bk_r, z, partner).wait()
    rows = back[:, :, 0:DS].reshape(LT, DS)
    out_ref[...] = (
        jnp.dot(whi[...], rows, preferred_element_type=F32)
        + jnp.dot(wlo[...], rows, preferred_element_type=F32)
    ).astype(BF16)
    off = lax.broadcasted_iota(jnp.int32, (LT, 128), 0) - CAP * lax.broadcasted_iota(
        jnp.int32, (LT, 128), 1
    )
    route = back[:, :, DS : DS + 128].reshape(LT, 128).astype(F32)
    route = jnp.where((off >= 0) & (off < CAP), route, 0.0).astype(BF16)
    vt = jnp.dot(onehot[...], route, preferred_element_type=F32).T
    for k in range(TOPK):
        gp_ref[k : k + 1, :] = jnp.sum(
            jnp.where(ids_ref[k : k + 1, :] == r128, vt, 0.0), axis=0, keepdims=True
        )

    for d in range(2):
        for s in range(4):
            zsend(d, s).wait_send()
    rcopy(idsall.at[1:16], idsall.at[1:16], ids_s, ids_r, z, a1p).wait_send()
    for d in range(2):
        rcopy(tok.at[0], tok.at[1], st1_s.at[d], tok_r.at[1, 0], z, a1p).wait_send()
    fwd1_hi.wait_send()
    fwd1_lo.wait_send()
    for mi in range(4):
        for d in range(2):
            rcopy(tok.at[mi], tok.at[5], st2_s.at[mi, d], tok_r.at[5, 0], z, a2p).wait_send()
    for u in range(8):
        rcopy(tok.at[4, lo], tok.at[12, lo], fw2_s.at[u], tok_r.at[12, 0], z, a2p).wait_send()
    for pair in range(2):
        for ee in range(2):
            dsend(3, pair, ee).wait_send()
    for buf in range(2):
        for ee in range(2):
            rs_wait_send(buf, ee)


def local(grad_out, probs, expert_ids, w_gate, w_up, w_down, saved_gate, saved_up):
    D, F, S = w_gate.shape[2], w_gate.shape[1], saved_gate.shape[2]
    DS = D // NZ
    vm = pl.BlockSpec(memory_space=pltpu.VMEM)
    hbm = pl.BlockSpec(memory_space=pl.ANY)
    dma = pltpu.SemaphoreType.DMA
    out, gp = pl.pallas_call(
        kernel,
        out_shape=(
            jax.ShapeDtypeStruct((TB, DS), BF16),
            jax.ShapeDtypeStruct((TOPK, TB), F32),
        ),
        in_specs=[vm, vm] + [hbm] * 6,
        out_specs=(vm, vm),
        scratch_shapes=[
            pltpu.VMEM((16, TB, D), BF16),
            pltpu.VMEM((2, F, D), BF16),
            pltpu.VMEM((2, F, D), BF16),
            pltpu.VMEM((2, F, D), BF16),
            pltpu.VMEM((2, F, S), BF16),
            pltpu.VMEM((2, F, S), BF16),
            pltpu.VMEM((2, 2, 48, D), BF16),
            pltpu.VMEM((4, 2, 2, 48, D), BF16),
            pltpu.VMEM((2, 2, 48, D), BF16),
            pltpu.VMEM((2, 2, NZ, 4, 48, DS), BF16),
            pltpu.VMEM((4, NZ - 1, 2, 4, 48, DS), BF16),
            pltpu.VMEM((32, 48, DS + 128), BF16),
            pltpu.VMEM((32, 48, DS + 128), BF16),
            pltpu.VMEM((16, TOPK, TB), jnp.int32),
            pltpu.VMEM((16, 8, TB), F32),
            pltpu.VMEM((16, 8, TB), F32),
            pltpu.VMEM((4, 8, 256), F32),
            pltpu.VMEM((4, NZ - 1, 8, 256), F32),
            pltpu.VMEM((2, 4, 48, 128), F32),
            pltpu.VMEM((TB, 1536), BF16),
            pltpu.VMEM((TB, 1536), BF16),
            pltpu.VMEM((TB, 1536), BF16),
            pltpu.VMEM((2, 192, F), BF16),
            pltpu.VMEM((2, 192, F), BF16),
            dma((6,)),
            dma,
            dma((2, 4)),
            dma((2, 4)),
            dma,
            dma,
            dma((2,)),
            dma((2,)),
            dma((4, 2)),
            dma((8,)),
            dma((16, 2)),
            dma((2, 2)),
            dma((4, 2, 2)),
            dma((2, 2)),
            dma((4, NZ - 1, 2, 4)),
            dma((4,)),
            dma((4,)),
            dma,
            dma,
        ],
        compiler_params=pltpu.CompilerParams(
            collective_id=0, has_side_effects=True, vmem_limit_bytes=67043328
        ),
    )(expert_ids.T, probs.T, grad_out, w_gate, w_up, w_down, saved_gate, saved_up)
    return out, gp.astype(BF16).T


def solution(mesh):
    placed = (
        P("expert", "section"),
        P("expert", None),
        P("expert", None),
        P("expert", "section", None),
        P("expert", "section", None),
        P("expert", "section", None),
        P("expert", "section", None),
        P("expert", "section", None),
    )
    return jax.shard_map(
        local,
        mesh=mesh,
        in_specs=placed,
        out_specs=(P("expert", "section"), P("expert", None)),
        check_vma=False,
    )
```

time: 457 us -> 200 us (0.44)
  Pallas kernels: 0 us -> 196 us
  blocking collectives: 167 us -> 0 us
  waiting for transfers between devices: 124 us -> 0 us
  local copies, waits for them, and re-layouts: 60.9 us -> 1.57 us
  matrix products: 39.4 us -> 0 us
  other arithmetic: 34.4 us -> 1.27 us
  starting transfers between devices: 14.5 us -> 0 us
  between operations: 14.2 us -> 0.64 us
    pallas_call x0 -> x1, Pallas kernels: none -> 196 us  [local(): pl.pallas_call(kernel, out_shape=(jax.ShapeDtypeStruct((TB, DS), BF16), j...]
    all_to_all x1 -> x0, blocking collectives: 153 us -> none  [local(): lax.all_to_all(outgoing, 'expert', split_axis=0, concat_axis=1, tiled=True)]
    reduce_scatter x1 -> x0, waiting for transfers between devices: 109 us -> none  [local(): lax.psum_scatter(term.astype(jnp.bfloat16), 'section', scatter_dimension=...]
    dot_general x3 -> x0, matrix products: 39.4 us -> none  [the longest x1 16.5 us: local(): jnp.einsum('efc,efs->esc', w_up, up_grad, preferred_element_type=jnp.floa...]
    gather x3 -> x0, local copies, waits for them, and re-layouts: 36.9 us -> none  [the longest x1 23.4 us: local(): outgoing = padded[table].reshape(expert_count, capacity, full_rows.shape[1])]
    another operation x3 -> x0, other arithmetic: 31 us -> none
    all_to_all x2 -> x0, waiting for transfers between devices: 14.9 us -> none  [the longest x1 14.9 us: local(): lax.all_to_all(shares, 'expert', split_axis=1, concat_axis=0, tiled=True)]
    all_to_all x2 -> x0, starting transfers between devices: 14.4 us -> none  [the longest x1 7.61 us: local(): lax.all_to_all(shares, 'expert', split_axis=1, concat_axis=0, tiled=True)]
  transfers between devices with their start and end apart: 4 -> 0, of which waited for: 2 -> 0; matrix products, arithmetic and copies ran while one was open for 11% -> 0% of each run, Pallas kernels for 0% -> 0%
where the time goes in v1:
time: 200 us; the launch traced here: 199 us
  Pallas kernels  196 us (98%)
    pallas_call x1, Pallas kernels, local(): pl.pallas_call(kernel, out_shape=(jax.ShapeDtypeStruct((TB, DS), BF16), j...  196 us

profile of v1, /device:TPU:1, one launch (start us, length us, event | category | flops | bytes accessed | tf_op | source)
XLA Modules:
  0.0 199.4 jit_solution(1777589437444174434)
XLA Ops:
  0.6 196.0 %shard_map.95 = (bf16[128,512]{1,0:T(8,128)(2,1)}, f32[8,128]{1,0:T(8,128)}) custom-call(s32[8,128]{1,0:T(8,128)} %bitcast.4, f32[8,128]{1,0:T(8,128)} %bitcast.5, bf16[128,512]{1,0:T(8,128)(2,1)} %x_hbm.1, bf16[2,192,4096]{2,1,0:T(8,128)(2,1)} %wg_hbm.1, bf16[2,192,4096]{2,1,0:T(8,128)(2,1)} %wu_hbm.1, bf16[2,192,4096]{2,1,0:T(8,128)(2,1)} %wd_hbm.1, ...), custom_call_target="tpu_custom_call" | custom-call | tf_op jit(solution)/shard_map/pallas_call | solution.py:512
  196.6 1.3 convert_bitcast_fusion
  197.9 1.6 copy.11

commit v2 on v1

v2 whole, which is shorter than its diff:
```python
import jax
import jax.numpy as jnp
from jax import lax
from jax.experimental import pallas as pl
from jax.experimental.pallas import tpu as pltpu
from jax.sharding import PartitionSpec as P

TOPK = 8
NZ = 8
CAP = 24
TB = 128
MESH = pl.DeviceIdType.MESH
F32 = jnp.float32
BF16 = jnp.bfloat16


def kernel(
    ids_ref, probs_ref, x_hbm, wg_hbm, wu_hbm, wd_hbm, sg_hbm, su_hbm,
    out_ref, gp_ref,
    tok, wgu, wd, sg, su, down, dpar, sendbuf, part, rbuf, fin, back,
    idsall, masks, codes, rown, rrecv, rcol, whi, wlo, onehot, gus,
    ld_sem, x_sem, zs_sem, zr_sem, ids_s, ids_r, st1_s, fw1_s, st2_s, fw2_s, tok_r,
    dp_s, dp_r, rs_s, rs_r, rt_s, rt_r, bk_s, bk_r,
):
    z = lax.axis_index("section")
    e = lax.axis_index("expert")
    x, y, c = e // 8, (e // 2) % 4, e % 2
    partner = e + 1 - 2 * c
    zp, zm = (z + 1) % NZ, (z + NZ - 1) % NZ
    D = tok.shape[2]
    DS = D // NZ
    F = wd.shape[1]

    def dev(cc, i, j):
        ax = (x * (1 - cc) + y * cc + i) % 4
        ay = (y * (1 - cc) + x * cc + j) % 4
        return ((ax * (1 - cc) + ay * cc) * 4 + (ay * (1 - cc) + ax * cc)) * 2 + cc

    def gray(m):
        return m + (m // 2) * (1 - 2 * (m % 2))

    def place(n):
        k, m = n // 4, n % 4
        mid = (k * (3 - k)) // 2
        v = 2 * ((k + 2) % 3) + m // 2
        i = gray(m) * (1 - mid) + gray(v) * mid
        j = 2 * (k // 3) * (1 - mid) + (1 + 2 * (m % 2)) * mid
        return i, j

    def rcopy(src, dst, ssem, rsem, zz, ee):
        return pltpu.make_async_remote_copy(
            src_ref=src, dst_ref=dst, send_sem=ssem, recv_sem=rsem,
            device_id=(zz, ee), device_id_type=MESH,
        )

    def cols(q):
        return pl.ds(pl.multiple_of(q * DS, DS), DS)

    xcopy = pltpu.make_async_copy(x_hbm, tok.at[0, :, cols(z)], x_sem)
    xcopy.start()
    loads = [
        pltpu.make_async_copy(a, b, ld_sem.at[n])
        for n, (a, b) in enumerate(
            ((sg_hbm, sg), (su_hbm, su), (wd_hbm, wd), (wg_hbm, wgu.at[:, 0:F]), (wu_hbm, wgu.at[:, F : 2 * F]))
        )
    ]
    idcopy = pltpu.make_async_copy(ids_ref, idsall.at[0], ld_sem.at[5])
    idcopy.start()

    barrier = pltpu.get_barrier_semaphore()

    def greet_z(n, carry):
        pl.semaphore_signal(barrier, inc=1, device_id=((z + n) % NZ, e), device_id_type=MESH)
        return carry

    def greet_e(n, carry):
        pl.semaphore_signal(barrier, inc=1, device_id=(z, (e + n) % 32), device_id_type=MESH)
        return carry

    lax.fori_loop(1, NZ, greet_z, 0)
    lax.fori_loop(1, 32, greet_e, 0)
    pl.semaphore_wait(barrier, NZ - 1 + 31)

    xcopy.wait()
    idcopy.wait()

    a1p, a1m = dev(c, 1, 0), dev(c, 3, 0)
    a2p, a2m = dev(c, 0, 1), dev(c, 0, 3)
    half = TB // 2

    lo, hi = pl.ds(0, half), pl.ds(half, half)

    def zhalf(q, d, s, h):
        rows = pl.ds(h * half, half)
        return rcopy(
            tok.at[0, rows, cols(q)], tok.at[0, rows, cols(q)], zs_sem.at[d, s, h],
            zr_sem.at[d, s, h], zp if d == 0 else zm, e,
        )

    def zsend(d, s, h):
        return zhalf((z + NZ - s) % NZ if d == 0 else (z + s) % NZ, d, s, h)

    def zrecv(d, s, h):
        return zhalf((z + NZ - 1 - s) % NZ if d == 0 else (z + 1 + s) % NZ, d, s, h)

    def first(q):
        for n, slot, ssem, to in (
            (0, 2, st1_s.at[0], a1p), (1, 1, st1_s.at[1], a1m),
            (2, 5, st2_s.at[0, 0], a2p), (3, 4, st2_s.at[0, 1], a2m),
        ):
            rcopy(tok.at[0, :, cols(q)], tok.at[slot, :, cols(q)], ssem, tok_r.at[slot, 0], z, to).start()

    for h in range(2):
        for d in range(2):
            zsend(d, 0, h).start()

    def send_ids(n, carry):
        i, j = n // 4, n % 4
        mi, jj = gray((4 - i) % 4), (4 - j) % 4
        odd = jj % 2
        slot = (1 - odd) * (6 * jj + mi) + odd * (4 + 2 * mi + jj // 2)
        rcopy(idsall.at[0], idsall.at[slot], ids_s, ids_r, z, dev(c, i, j)).start()
        return carry

    first(z)
    lax.fori_loop(1, 16, send_ids, 0)
    for cp in loads:
        cp.start()
    for s in range(1, 4):
        for h in range(2):
            for d in range(2):
                zrecv(d, s - 1, h).wait_recv()
                if s < 3 or h == d:
                    zsend(d, s, h).start()
        first((z + NZ - s) % NZ)
        first((z + s) % NZ)
    zrecv(0, 3, 0).wait_recv()
    zrecv(1, 3, 1).wait_recv()
    first((z + 4) % NZ)

    rcopy(idsall.at[1:16], idsall.at[1:16], ids_s, ids_r, z, a1p).wait_recv()
    row8 = lax.broadcasted_iota(jnp.int32, (8, TB), 0)
    mine = jnp.where(row8 < 2, 2 * e + row8, 2 * partner + row8 - 2)
    mine = jnp.where(row8 < 4, mine, -1)

    def mask_of(n, carry):
        table = idsall[n]
        hit = jnp.zeros((8, TB), F32)
        for k in range(TOPK):
            hit = hit + jnp.where(table[k : k + 1, :] == mine, 1.0, 0.0)
        masks[n] = hit
        return carry

    lax.fori_loop(0, 16, mask_of, 0)
    r128 = lax.broadcasted_iota(jnp.int32, (TB, TB), 0)
    l128 = lax.broadcasted_iota(jnp.int32, (TB, TB), 1)
    tri = jnp.where(r128 < l128, 1.0, 0.0).astype(BF16)
    mk = masks[...].reshape(TB, TB)
    ps = jnp.dot(mk.astype(BF16), tri, preferred_element_type=F32)
    codes[...] = jnp.where(mk > 0.5, ps, -1.0).reshape(16, 8, TB)

    LT = onehot.shape[1]

    def weights():
        hit = jnp.zeros((TB, TB), F32)
        pe = jnp.zeros((TB, TB), F32)
        for k in range(TOPK):
            same = ids_ref[k : k + 1, :] == r128
            hit = hit + jnp.where(same, 1.0, 0.0)
            pe = pe + jnp.where(same, probs_ref[k : k + 1, :], 0.0)
        ps = jnp.dot(hit.astype(BF16), tri, preferred_element_type=F32)
        code_te = jnp.where(hit > 0.5, ps, -1.0).T.astype(BF16)
        prob_te = pe.T
        prob_hi = prob_te.astype(BF16)
        prob_lo = (prob_te - prob_hi.astype(F32)).astype(BF16)
        for lt in range(0, LT, 512):
            el = lax.broadcasted_iota(jnp.int32, (TB, 512), 0)
            ll = lax.broadcasted_iota(jnp.int32, (TB, 512), 1) + lt
            off = ll - CAP * el
            spread = jnp.where((off >= 0) & (off < CAP), 1.0, 0.0)
            s_of = jnp.sum(spread * off.astype(F32), axis=0, keepdims=True)
            spread = spread.astype(BF16)
            code_l = jnp.dot(code_te, spread, preferred_element_type=F32)
            prob_l = jnp.dot(prob_hi, spread, preferred_element_type=F32) + jnp.dot(
                prob_lo, spread, preferred_element_type=F32
            )
            oh = jnp.where(jnp.abs(code_l - s_of) < 0.5, 1.0, 0.0)
            w = oh * prob_l
            w_hi = w.astype(BF16)
            onehot[:, lt : lt + 512] = oh.astype(BF16)
            whi[:, lt : lt + 512] = w_hi
            wlo[:, lt : lt + 512] = (w - w_hi.astype(F32)).astype(BF16)

    def second(mi):
        rcopy(tok.at[mi], tok.at[5 + 2 * mi], st2_s.at[mi, 0], tok_r.at[5 + 2 * mi, 0], z, a2p).start()
        rcopy(tok.at[mi], tok.at[4 + 2 * mi], st2_s.at[mi, 1], tok_r.at[4 + 2 * mi, 0], z, a2m).start()

    def whole(n):
        return rcopy(tok.at[n], tok.at[n], st2_s.at[0, 0], tok_r.at[n, 0], z, a2p)

    def half_of(n, h):
        rows = pl.ds(h * half, half)
        return rcopy(tok.at[n, rows], tok.at[n, rows], st2_s.at[0, 0], tok_r.at[n, h], z, a2p)

    fwd1_hi = rcopy(tok.at[1, hi], tok.at[3, hi], fw1_s.at[1], tok_r.at[3, 1], z, a1m)
    fwd1_lo = rcopy(tok.at[2, lo], tok.at[3, lo], fw1_s.at[0], tok_r.at[3, 0], z, a1p)
    whole(1).wait_recv()
    fwd1_hi.start()
    second(1)
    whole(2).wait_recv()
    fwd1_lo.start()
    second(2)
    for cp in loads:
        cp.wait()

    def arrive(it):
        @pl.when(it == 1)
        def _():
            half_of(3, 0).wait_recv()
            half_of(3, 1).wait_recv()
            second(3)

        @pl.when((it >= 2) & (it <= 5))
        def _():
            for a in range(2):
                n = 2 * it + a
                whole(n).wait_recv()
                rows = pl.ds((1 - a) * half, half)
                n2 = 10 + it
                rcopy(
                    tok.at[n, rows], tok.at[n2, rows], fw2_s.at[n - 4], tok_r.at[n2, 1 - a],
                    z, a2p if a == 1 else a2m,
                ).start()

        @pl.when(it >= 6)
        def _():
            for a in range(2):
                for h in range(2):
                    half_of(2 * it + a, h).wait_recv()

    s24 = lax.broadcasted_iota(jnp.int32, (CAP, TB), 0).astype(F32)

    def dsend(k, ee):
        return rcopy(
            sendbuf.at[k % 2, ee], dpar.at[k, ee], dp_s.at[k % 2, ee], dp_r.at[k, ee],
            z, partner,
        )

    def dispatch(it):
        n0 = 2 * it
        buf = it % 2
        code0, code1 = codes[n0], codes[n0 + 1]
        zero = jnp.zeros((CAP, TB), F32)
        blocks = []
        for q in range(4):
            b0 = jnp.where(jnp.abs(code0[q : q + 1, :] - s24) < 0.5, 1.0, 0.0)
            b1 = jnp.where(jnp.abs(code1[q : q + 1, :] - s24) < 0.5, 1.0, 0.0)
            blocks.append(jnp.concatenate([b0, zero], axis=1))
            blocks.append(jnp.concatenate([zero, b1], axis=1))
        pick = jnp.concatenate(blocks, axis=0).astype(BF16)

        @pl.when(it >= 2)
        def _():
            dsend(it, 0).wait_send()
            dsend(it, 1).wait_send()

        def tile(t, carry):
            cs = pl.ds(pl.multiple_of(t * 512, 512), 512)
            rows = tok[pl.ds(n0, 2), :, cs].reshape(2 * TB, 512)
            got = jnp.dot(pick, rows, preferred_element_type=F32).astype(BF16)
            down[0, :, cs] = got[0:48]
            down[1, :, cs] = got[48:96]
            sendbuf[buf, 0, :, cs] = got[96:144]
            sendbuf[buf, 1, :, cs] = got[144:192]
            return carry

        lax.fori_loop(0, D // 512, tile, 0)
        dsend(it, 0).start()
        dsend(it, 1).start()

    NT = (((1,), (1,)), ((), ()))

    def saved_rows(it):
        base = lax.broadcasted_iota(jnp.int32, (CAP, sg.shape[2]), 1) - lax.broadcasted_iota(
            jnp.int32, (CAP, sg.shape[2]), 0
        )
        blocks = []
        for o in range(2):
            cc = c if o == 0 else 1 - c
            for a in range(2):
                i, j = place(2 * it + a)
                blocks.append(jnp.where(base == dev(cc, i, j) * CAP, 1.0, 0.0))
        return jnp.concatenate(blocks, axis=0).astype(BF16)

    def hidden(it, ee, perm, eye):
        acc = jnp.zeros((96, F), F32)
        for kt in range(0, D, 512):
            rows = jnp.concatenate(
                [
                    down[ee, :, kt : kt + 512],
                    dpar[it, ee, :, kt : kt + 512],
                ],
                axis=0,
            )
            acc = acc + lax.dot_general(
                rows, wd[ee, :, kt : kt + 512], NT, preferred_element_type=F32
            )
        g = lax.dot_general(perm, sg[ee], NT, preferred_element_type=F32)
        u = lax.dot_general(perm, su[ee], NT, preferred_element_type=F32)
        s = 1.0 / (1.0 + jnp.exp(-g))
        silu = g * s
        router = jnp.sum(silu * u * acc, axis=1, keepdims=True)
        rown[it, ee : ee + 1, 0:96] = jnp.sum(router * eye, axis=0, keepdims=True)
        gus[ee, :, 0:F] = (acc * u * s * (1.0 + g * (1.0 - s))).astype(BF16)
        gus[ee, :, F : 2 * F] = (acc * silu).astype(BF16)

    def eye_of():
        return jnp.where(
            lax.broadcasted_iota(jnp.int32, (96, 96), 0)
            == lax.broadcasted_iota(jnp.int32, (96, 96), 1),
            1.0,
            0.0,
        )

    def rs_wait_send(buf):
        rcopy(
            rbuf.at[0], rbuf.at[0], rs_s.at[buf], rs_r.at[0, 0, 0], zp, e,
        ).wait_send()

    def partial(it, ee):
        buf = it % 3

        if ee == 0:
            @pl.when(it >= 3)
            def _():
                rs_wait_send(buf)

        gu = gus[ee]

        def tile(t, carry):
            cs = cols(t)
            v = jnp.dot(gu, wgu[ee, :, cs], preferred_element_type=F32)
            part[buf, ee, t] = v.astype(BF16)
            return carry

        lax.fori_loop(0, NZ, tile, 0)

    def router_copy(k, n):
        return rcopy(rown.at[k], rrecv.at[k, n - 1], rt_s.at[k], rt_r.at[k], (z + n) % NZ, e)

    def send_router(it):
        def go(n, carry):
            router_copy(it, n).start()
            return carry

        lax.fori_loop(1, NZ, go, 0)

    def work(it, h):
        if h == 0:
            for ee in range(2):
                dsend(it, ee).wait_recv()
            hidden(it, 0, saved_rows(it), eye_of())
        elif h == 1:
            hidden(it, 1, saved_rows(it), eye_of())
            send_router(it)
        elif h == 2:
            partial(it, 0)
        else:
            partial(it, 1)

    def fetch(it):
        arrive(it)
        dispatch(it)

    def rs_copy(k, s, d, ee):
        t = (z + 4 - s) % NZ if d == 0 else (z + 4 + s) % NZ
        n = 2 * s - 1 + ee if s else 0
        return rcopy(
            part.at[k % 3, ee, t], rbuf.at[k, d, n], rs_s.at[k % 3],
            rs_r.at[k, d, n], zp if d == 0 else zm, e,
        ), t, n

    def ring(k, s):
        order = [(ee, d) for ee in range(2) for d in range(2)]
        if s == 0:
            order = [(0, 0), (1, 1)]
        elif s == 1:
            order = [(1, 0), (0, 1), (0, 0), (1, 1)]
        for ee, d in order:
            cp, t, n = rs_copy(k, s, d, ee)
            if s > 1 or (s == 1 and ee == d):
                before, _, m = rs_copy(k, s - 1, d, ee)
                before.wait_recv()
                part[k % 3, ee, t] = (
                    part[k % 3, ee, t].astype(F32) + rbuf[k, d, m].astype(F32)
                ).astype(BF16)
            cp.start()

    def message(n, cc, i, j):
        return rcopy(fin.at[n], back.at[e], bk_s, bk_r, z, dev(cc, i, j))

    def finish(k):
        rcopy(rrecv.at[k], rrecv.at[k], rt_s.at[k], rt_r.at[k], zp, e).wait()
        rows = rown[k]
        for n in range(NZ - 1):
            rows = rows + rrecv[k, n]
        eye = eye_of()
        for ee in range(2):
            col = jnp.sum(rows[ee : ee + 1, 0:96] * eye, axis=1, keepdims=True)
            rcol[ee] = jnp.broadcast_to(col, (96, 128))
        got = []
        for ee in range(2):
            total = part[k % 3, ee, z].astype(F32)
            for d in range(2):
                last, _, m = rs_copy(k, 3, d, ee)
                last.wait_recv()
                total = total + rbuf[k, d, m].astype(F32)
            got.append(total)
        for o in range(2):
            cc = c if o == 0 else 1 - c
            for a in range(2):
                n = 4 * k + 2 * o + a
                lo_, hi_ = 48 * o + 24 * a, 48 * o + 24 * a + 24
                fin[n, :, 0:DS] = jnp.concatenate([got[0][lo_:hi_], got[1][lo_:hi_]], axis=0).astype(BF16)
                fin[n, :, DS : DS + 128] = jnp.concatenate(
                    [rcol[0, lo_:hi_], rcol[1, lo_:hi_]], axis=0
                ).astype(BF16)
                i, j = place(2 * k + a)
                if o == 0 and a == 0:
                    @pl.when(k == 0)
                    def _():
                        back[e] = fin[n]

                    @pl.when(k > 0)
                    def _():
                        message(n, cc, i, j).start()
                else:
                    message(n, cc, i, j).start()

    def step(it, carry):
        def when(lo_, hi_, fn, *args):
            @pl.when((it >= lo_) & (it <= hi_))
            def _():
                fn(*args)

        when(2, 9, ring, it - 2, 2)
        when(3, 10, finish, it - 3)
        when(9, 9, weights)
        when(1, 8, ring, it - 1, 1)
        when(0, 7, work, it, 0)
        when(0, 7, work, it, 1)
        when(0, 7, work, it, 2)
        when(2, 9, ring, it - 2, 3)
        when(0, 7, work, it, 3)
        when(0, 7, ring, it, 0)
        when(0, 6, fetch, it + 1)
        return carry

    dispatch(0)
    lax.fori_loop(0, 11, step, 0)

    rcopy(back.at[0:31], back.at[0:31], bk_s, bk_r, z, partner).wait()
    rows = back[:, :, 0:DS].reshape(LT, DS)
    out_ref[...] = (
        jnp.dot(whi[...], rows, preferred_element_type=F32)
        + jnp.dot(wlo[...], rows, preferred_element_type=F32)
    ).astype(BF16)
    off = lax.broadcasted_iota(jnp.int32, (LT, 128), 0) - CAP * lax.broadcasted_iota(
        jnp.int32, (LT, 128), 1
    )
    route = back[:, :, DS : DS + 128].reshape(LT, 128).astype(F32)
    route = jnp.where((off >= 0) & (off < CAP), route, 0.0).astype(BF16)
    vt = jnp.dot(onehot[...], route, preferred_element_type=F32).T
    for k in range(TOPK):
        gp_ref[k : k + 1, :] = jnp.sum(
            jnp.where(ids_ref[k : k + 1, :] == r128, vt, 0.0), axis=0, keepdims=True
        )

    for d in range(2):
        for s in range(4):
            for h in range(2):
                if s < 3 or h == d:
                    zsend(d, s, h).wait_send()
    rcopy(idsall.at[1:16], idsall.at[1:16], ids_s, ids_r, z, a1p).wait_send()
    for d in range(2):
        rcopy(tok.at[0], tok.at[1], st1_s.at[d], tok_r.at[1, 0], z, a1p).wait_send()
    fwd1_hi.wait_send()
    fwd1_lo.wait_send()
    for mi in range(4):
        for d in range(2):
            rcopy(tok.at[mi], tok.at[5], st2_s.at[mi, d], tok_r.at[5, 0], z, a2p).wait_send()
    for u in range(8):
        rcopy(tok.at[4, lo], tok.at[12, lo], fw2_s.at[u], tok_r.at[12, 0], z, a2p).wait_send()
    for k in range(2):
        for ee in range(2):
            dsend(k, ee).wait_send()
    for buf in range(3):
        rs_wait_send(buf)


def local(grad_out, probs, expert_ids, w_gate, w_up, w_down, saved_gate, saved_up):
    D, F, S = w_gate.shape[2], w_gate.shape[1], saved_gate.shape[2]
    DS = D // NZ
    vm = pl.BlockSpec(memory_space=pltpu.VMEM)
    hbm = pl.BlockSpec(memory_space=pl.ANY)
    dma = pltpu.SemaphoreType.DMA
    out, gp = pl.pallas_call(
        kernel,
        out_shape=(
            jax.ShapeDtypeStruct((TB, DS), BF16),
            jax.ShapeDtypeStruct((TOPK, TB), F32),
        ),
        in_specs=[vm, vm] + [hbm] * 6,
        out_specs=(vm, vm),
        scratch_shapes=[
            pltpu.VMEM((16, TB, D), BF16),
            pltpu.VMEM((2, 2 * F, D), BF16),
            pltpu.VMEM((2, F, D), BF16),
            pltpu.VMEM((2, F, S), BF16),
            pltpu.VMEM((2, F, S), BF16),
            pltpu.VMEM((2, 48, D), BF16),
            pltpu.VMEM((8, 2, 48, D), BF16),
            pltpu.VMEM((2, 2, 48, D), BF16),
            pltpu.VMEM((3, 2, NZ, 96, DS), BF16),
            pltpu.VMEM((8, 2, NZ - 1, 96, DS), BF16),
            pltpu.VMEM((32, 48, DS + 128), BF16),
            pltpu.VMEM((32, 48, DS + 128), BF16),
            pltpu.VMEM((16, TOPK, TB), jnp.int32),
            pltpu.VMEM((16, 8, TB), F32),
            pltpu.VMEM((16, 8, TB), F32),
            pltpu.VMEM((8, 8, 128), F32),
            pltpu.VMEM((8, NZ - 1, 8, 128), F32),
            pltpu.VMEM((2, 96, 128), F32),
            pltpu.VMEM((TB, 1536), BF16),
            pltpu.VMEM((TB, 1536), BF16),
            pltpu.VMEM((TB, 1536), BF16),
            pltpu.VMEM((2, 96, 2 * F), BF16),
            dma((6,)),
            dma,
            dma((2, 4, 2)),
            dma((2, 4, 2)),
            dma,
            dma,
            dma((2,)),
            dma((2,)),
            dma((4, 2)),
            dma((8,)),
            dma((16, 2)),
            dma((2, 2)),
            dma((8, 2)),
            dma((3,)),
            dma((8, 2, NZ - 1)),
            dma((8,)),
            dma((8,)),
            dma,
            dma,
        ],
        compiler_params=pltpu.CompilerParams(
            collective_id=0, has_side_effects=True, vmem_limit_bytes=67043328
        ),
    )(expert_ids.T, probs.T, grad_out, w_gate, w_up, w_down, saved_gate, saved_up)
    return out, gp.astype(BF16).T


def solution(mesh):
    placed = (
        P("expert", "section"),
        P("expert", None),
        P("expert", None),
        P("expert", "section", None),
        P("expert", "section", None),
        P("expert", "section", None),
        P("expert", "section", None),
        P("expert", "section", None),
    )
    return jax.shard_map(
        local,
        mesh=mesh,
        in_specs=placed,
        out_specs=(P("expert", "section"), P("expert", None)),
        check_vma=False,
    )
```

time: 200 us -> 193 us (0.965)
  Pallas kernels: 196 us -> 190 us
    pallas_call x1, Pallas kernels: 196 us -> 190 us  [local(): pl.pallas_call(kernel, out_shape=(jax.ShapeDtypeStruct((TB, DS), BF16), j...]
where the time goes in v2:
time: 193 us
  Pallas kernels  190 us (98%)
    pallas_call x1, Pallas kernels, local(): pl.pallas_call(kernel, out_shape=(jax.ShapeDtypeStruct((TB, DS), BF16), j...  190 us

profile of v2, /device:TPU:1, one launch (start us, length us, event | category | flops | bytes accessed | tf_op | source)
XLA Modules:
  0.0 193.2 jit_solution(6378747625913043453)
XLA Ops:
  0.6 189.7 %shard_map.95 = (bf16[128,512]{1,0:T(8,128)(2,1)}, f32[8,128]{1,0:T(8,128)}) custom-call(s32[8,128]{1,0:T(8,128)} %bitcast.4, f32[8,128]{1,0:T(8,128)} %bitcast.5, bf16[128,512]{1,0:T(8,128)(2,1)} %x_hbm.1, bf16[2,192,4096]{2,1,0:T(8,128)(2,1)} %wg_hbm.1, bf16[2,192,4096]{2,1,0:T(8,128)(2,1)} %wu_hbm.1, bf16[2,192,4096]{2,1,0:T(8,128)(2,1)} %wd_hbm.1, ...), custom_call_target="tpu_custom_call" | custom-call | tf_op jit(solution)/shard_map/pallas_call | solution.py:507
  190.3 1.3 convert_bitcast_fusion
  191.6 1.6 copy.11
